TPU v7x, 512 devices: a whole 4x8x8 slice. The times are simulated.
512 devices in a mesh: dp: 16 (over y_lo, z), gx: 8 (over x, core), gy: 4 (over y_hi).
Axes of the slice: x: 4, y: 8 (y_hi: 4, y_lo: 2; y = y_hi * 2 + y_lo), z: 8, core: 2. Of those that a mesh axis runs over, the one named last changes fastest.
Arguments:
- fields: bfloat16 [16, 20, 32, 16384], P('dp', None, None, ('gx', 'gy')), may hold values from -6 to 6
- cotangent: bfloat16 [16, 20, 32, 16384], P('dp', None, None, ('gx', 'gy')), may hold values from -6 to 6
- mix_weight: bfloat16 [20, 20], replicated, may hold values from -1.25 to 1.25
- spectral_weight: bfloat16 [288, 2, 20, 20], P(('gx', 'gy')), may hold values from -1 to 1
Outputs:
- output: bfloat16 [16, 20, 32, 16384], P('dp', None, None, ('gx', 'gy'))
- spectral_grad: float32 [288, 2, 20, 20], P(('gx', 'gy'))
- mixing_grad: float32 [20, 20], replicated
All inputs are finite; a program needn't handle non-finite values.
Results may differ from a plain program's by a relative error of at most 0.0031.
Values may be sent and summed in bfloat16 or wider, within the bound.
A program may use at most 64 MiB of HBM per device.

v0:
```python
import math
import jax
import jax.numpy as jnp
from jax import lax
from jax.sharding import PartitionSpec as P

NX = 128
NY = 128
KX = 24
KY = 12
P_SIZE = 32
MODES = 288
HI = lax.Precision.HIGHEST


def gelu_value(h):
    k = math.sqrt(2.0 / math.pi)
    t = jnp.tanh(k * (h + 0.044715 * h * h * h))
    return 0.5 * h * (1.0 + t)


def gelu_slope(h):
    k = math.sqrt(2.0 / math.pi)
    t = jnp.tanh(k * (h + 0.044715 * h * h * h))
    return 0.5 * (1.0 + t) + 0.5 * h * (1.0 - t * t) * k * (1.0 + 3.0 * 0.044715 * h * h)


def axis_table(waves, n):
    cells = jnp.arange(n, dtype=jnp.int32)
    angle = 2.0 * math.pi / n * (waves[:, None] * cells[None, :] % n).astype(jnp.float32)
    return (jnp.cos(angle), jnp.sin(angle))


def tables():
    index = jnp.arange(KX, dtype=jnp.int32)
    waves_x = jnp.where(index < KX // 2, index, NX - KX + index)
    cos_x, sin_x = axis_table(waves_x, NX)
    cos_y, sin_y = axis_table(jnp.arange(KY, dtype=jnp.int32), NY)
    return (cos_x, sin_x, cos_y, sin_y)


def forward_dft(data, scale):
    cos_x, sin_x, cos_y, sin_y = tables()
    a_re = jnp.einsum("cpxy,ky->cpxk", data, cos_y, precision=HI)
    a_im = -jnp.einsum("cpxy,ky->cpxk", data, sin_y, precision=HI)
    s_re = jnp.einsum("cpxk,jx->jkcp", a_re, cos_x, precision=HI) + jnp.einsum(
        "cpxk,jx->jkcp", a_im, sin_x, precision=HI
    )
    s_im = jnp.einsum("cpxk,jx->jkcp", a_im, cos_x, precision=HI) - jnp.einsum(
        "cpxk,jx->jkcp", a_re, sin_x, precision=HI
    )
    chans, planes = (data.shape[0], data.shape[1])
    return scale * jnp.stack(
        [s_re.reshape(MODES, chans, planes), s_im.reshape(MODES, chans, planes)], axis=1
    )


def inverse_dft(vals, scale):
    cos_x, sin_x, cos_y, sin_y = tables()
    chans, planes = (vals.shape[2], vals.shape[3])
    v_re = vals[:, 0].reshape(KX, KY, chans, planes)
    v_im = vals[:, 1].reshape(KX, KY, chans, planes)
    b_re = jnp.einsum("jkdp,jx->dpxk", v_re, cos_x, precision=HI) - jnp.einsum(
        "jkdp,jx->dpxk", v_im, sin_x, precision=HI
    )
    b_im = jnp.einsum("jkdp,jx->dpxk", v_re, sin_x, precision=HI) + jnp.einsum(
        "jkdp,jx->dpxk", v_im, cos_x, precision=HI
    )
    return scale * (
        jnp.einsum("dpxk,ky->dpxy", b_re, cos_y, precision=HI)
        - jnp.einsum("dpxk,ky->dpxy", b_im, sin_y, precision=HI)
    )


def spectral_mix(spec, weight):
    w = weight.astype(jnp.float32)
    v_re = jnp.einsum("mcp,mcd->mdp", spec[:, 0], w[:, 0], precision=HI) - jnp.einsum(
        "mcp,mcd->mdp", spec[:, 1], w[:, 1], precision=HI
    )
    v_im = jnp.einsum("mcp,mcd->mdp", spec[:, 0], w[:, 1], precision=HI) + jnp.einsum(
        "mcp,mcd->mdp", spec[:, 1], w[:, 0], precision=HI
    )
    return jnp.stack([v_re, v_im], axis=1)


def grads_of(spec, gspec):
    g_re = jnp.einsum("mcp,mdp->mcd", spec[:, 0], gspec[:, 0], precision=HI) + jnp.einsum(
        "mcp,mdp->mcd", spec[:, 1], gspec[:, 1], precision=HI
    )
    g_im = jnp.einsum("mcp,mdp->mcd", spec[:, 0], gspec[:, 1], precision=HI) - jnp.einsum(
        "mcp,mdp->mcd", spec[:, 1], gspec[:, 0], precision=HI
    )
    return jnp.stack([g_re, g_im], axis=1)


def to_planes(block):
    chans, planes, rows_x, full_y = block.shape
    size_x = lax.axis_size("gx")
    size_y = lax.axis_size("gy")
    moved = lax.all_to_all(
        lax.all_to_all(block, "gx", split_axis=1, concat_axis=2, tiled=True),
        "gy",
        split_axis=1,
        concat_axis=2,
        tiled=True,
    )
    own = moved.shape[1]
    moved = moved.reshape(chans, own, size_y, size_x, rows_x, full_y)
    moved = jnp.transpose(moved, (0, 1, 3, 2, 4, 5))
    return moved.reshape(chans, own, size_x * size_y * rows_x, full_y)


def to_cells(plane_block):
    chans, own, full_x, full_y = plane_block.shape
    size_x = lax.axis_size("gx")
    size_y = lax.axis_size("gy")
    rows_x = full_x // (size_x * size_y)
    moved = lax.all_to_all(
        lax.all_to_all(plane_block, "gx", split_axis=2, concat_axis=1, tiled=True),
        "gy",
        split_axis=2,
        concat_axis=1,
        tiled=True,
    )
    moved = moved.reshape(chans, size_y, size_x, own, rows_x, full_y)
    moved = jnp.transpose(moved, (0, 2, 1, 3, 4, 5))
    return moved.reshape(chans, size_x * size_y * own, rows_x, full_y)


def local(fields, cotangent, mix_weight, spectral_weight):
    flat = fields[0]
    grad_out = cotangent[0].astype(jnp.float32)
    chans, planes, cells = flat.shape
    rows_x = cells // NY
    norm_in = 1.0 / math.sqrt(NX * NY)
    norm_out = 1.0 / math.sqrt(MODES)
    samples = lax.axis_size("dp")
    mixed = jnp.einsum("cpq,cd->dpq", flat, mix_weight, preferred_element_type=jnp.float32)
    plane_field = to_planes(flat.reshape(chans, planes, rows_x, NY)).astype(jnp.float32)
    spec = forward_dft(plane_field, norm_in)
    full_weight = lax.all_gather(spectral_weight, ("gx", "gy"), axis=0, tiled=True)
    vals = spectral_mix(spec, full_weight)
    branch = to_cells(inverse_dft(vals, norm_out)).reshape(chans, planes, cells)
    pre = branch + mixed
    output = gelu_value(pre).astype(jnp.bfloat16).reshape(1, chans, planes, cells)
    back = (grad_out * gelu_slope(pre)).astype(jnp.bfloat16)
    local_mix = jnp.einsum("cpq,dpq->cd", flat, back, preferred_element_type=jnp.float32)
    mix_scale = 1.0 / math.sqrt(samples * P_SIZE * NX * NY)
    spec_scale = 1.0 / math.sqrt(samples * P_SIZE)
    plane_back = to_planes(back.reshape(chans, planes, rows_x, NY)).astype(jnp.float32)
    gspec = forward_dft(plane_back, norm_out)
    local_spec = grads_of(spec, gspec)
    share = lax.psum_scatter(local_spec, ("gx", "gy"), scatter_dimension=0, tiled=True)
    spectral_grad = lax.psum(share, "dp") * spec_scale
    mixing_grad = lax.psum(local_mix, ("dp", "gx", "gy")) * mix_scale
    return (output, spectral_grad, mixing_grad)


def solution(mesh):
    return jax.shard_map(
        local,
        mesh=mesh,
        in_specs=(
            P("dp", None, None, ("gx", "gy")),
            P("dp", None, None, ("gx", "gy")),
            P(),
            P(("gx", "gy"), None, None, None),
        ),
        out_specs=(P("dp", None, None, ("gx", "gy")), P(("gx", "gy"), None, None, None), P()),
        check_vma=False,
    )
```

profile of v0, /device:TPU:2, one launch (start us, length us, event | category | flops | bytes accessed | tf_op | source)
XLA Modules:
  0.0 713.6 jit_solution(4944024013968660867)
XLA Ops:
  7.2 1.6 reshape_squeeze.3
  8.8 1.1 copy.251
  9.9 10.0 %all-to-all-start = ((bf16[20,32,4,128]{3,2,0,1:T(4,128)(2,1)}), bf16[20,32,4,128]{3,2,0,1:T(4,128)(2,1)}, u32[]{:S(2)}, u32[]{:S(2)}) async-start(bf16[20,32,4,128]{3,2,0,1:T(4,128)(2,1)} %copy.251), calls=%async_computation | async-start | bytes 1310720 | tf_op jit(solution)/shard_map/all_to_all | solution.py:101
  19.9 112.9 %all_gather.3 = bf16[288,2,20,20]{3,1,2,0:T(2,128)(2,1)S(1)} all-gather(bf16[9,2,20,20]{3,1,2,0:T(2,128)(2,1)S(1)} %copy-done.5), channel_id=1, replica_groups=mesh['dp'=16,'gx'=8,'gy'=4] {'gx','gy'}, dimensions={0}, use_global_device_ids=true | all-gather | bytes 475200 | tf_op jit(solution)/shard_map/all_gather | solution.py:141
  132.7 1.3 copy.252
  134.4 0.9 copy.254
  135.2 4.8 all-to-all-start.1
  140.1 5.6 fusion.165
  145.7 6.4 copy.317
  152.1 4.7 copy.318
  156.8 1.9 all-to-all-done.1
  158.7 1.2 copy.255
  160.1 0.6 fusion.9
  160.8 0.6 convolution_bitcast_fusion
  161.4 0.9 fusion.33
  162.3 0.9 fusion.29
  163.3 0.9 fusion.15
  164.2 0.9 fusion.14
  166.9 0.4 fusion.41
  168.1 0.4 fusion.12
  168.9 2.2 fusion.24
  171.1 2.2 fusion.8
  173.3 1.3 copy.271
  174.7 20.8 %all_to_all.81 = f32[20,1,128,128]{3,1,0,2:T(1,128)S(1)} all-to-all(f32[20,1,128,128]{3,1,0,2:T(1,128)S(1)} %copy.271), channel_id=1, replica_groups=mesh['dp'=16,'gx'=8,'gy'=4] {'gx'}, dimensions={2} | all-to-all | bytes 2621440 | tf_op jit(solution)/shard_map/all_to_all | solution.py:119
  195.7 0.4 copy.273
  196.1 39.4 %all_to_all.82 = f32[20,8,16,128]{3,1,0,2:T(8,128)S(1)} all-to-all(f32[20,8,16,128]{3,1,0,2:T(8,128)S(1)} %copy.273), channel_id=1, replica_groups=mesh['dp'=16,'gx'=8,'gy'=4] {'gy'}, dimensions={2} | all-to-all | bytes 2621440 | tf_op jit(solution)/shard_map/all_to_all | solution.py:118
  235.4 0.8 copy.357
  236.3 0.5 reshape_reshape.3
  236.8 0.5 copy-done.4
  237.4 4.7 fusion.6
  242.4 14.0 %all_to_all.83 = bf16[20,32,4,128]{3,2,0,1:T(4,128)(2,1)S(1)} all-to-all(bf16[20,32,4,128]{3,2,0,1:T(4,128)(2,1)S(1)} %reshape.261), channel_id=1, replica_groups=mesh['dp'=16,'gx'=8,'gy'=4] {'gx'}, dimensions={1} | all-to-all | bytes 1310720 | tf_op jit(solution)/shard_map/all_to_all | solution.py:101
  256.8 22.2 %all_to_all.84 = bf16[20,4,32,128]{3,2,0,1:T(8,128)(2,1)S(1)} all-to-all(bf16[20,4,32,128]{3,2,0,1:T(8,128)(2,1)S(1)} %copy.282), channel_id=1, replica_groups=mesh['dp'=16,'gx'=8,'gy'=4] {'gy'}, dimensions={1} | all-to-all | bytes 1310720 | tf_op jit(solution)/shard_map/all_to_all | solution.py:100
  279.3 0.6 fusion.59
  280.0 0.6 fusion.63
  280.6 0.9 fusion.27
  281.6 0.9 fusion.35
  282.5 0.9 fusion.11
  283.4 0.9 fusion.10
  285.7 6.0 copy.290
  291.8 1.3 dynamic-slice
  293.8 1.0 copy.292
  294.8 0.7 convolution_bitcast_fusion.1
  295.5 107.2 %psum.15 = f32[20,20]{0,1:T(8,128)S(1)} all-reduce(f32[20,20]{0,1:T(8,128)S(1)} %convolution_bitcast_fusion.1), channel_id=1, replica_groups=mesh['dp'=16,'gx'=8,'gy'=4] {'dp','gx','gy'}, use_global_device_ids=true, to_apply=%region_2.3 | all-reduce | flops 400 | bytes 3200 | tf_op jit(solution)/shard_map/psum | solution.py:155
  402.7 0.7 copy.293
  403.4 233.1 %all-reduce.3.cloned.1.call-done = f32[288,2,20,20]{3,1,2,0:T(2,128)} async-done(((f32[288,2,20,20]{3,1,2,0:T(2,128)}), f32[288,2,20,20]{3,1,2,0:T(2,128)}) %all-reduce.3.cloned.1.call-update) | async-done | bytes 921616
  636.4 0.9 constant_dynamic-slice_fusion
  637.4 68.6 %psum.14 = f32[9,2,20,20]{3,1,2,0:T(2,128)S(1)} all-reduce(f32[9,2,20,20]{3,1,2,0:T(2,128)S(1)} %constant_dynamic-slice_fusion), channel_id=1, replica_groups=mesh['dp'=16,'gx'=8,'gy'=4] {'dp'}, use_global_device_ids=true, to_apply=%region_1.2 | all-reduce | flops 7200 | bytes 57600 | tf_op jit(solution)/shard_map/psum | solution.py:154
  706.0 0.8 broadcast_multiply_fusion
  (50 shorter events, 5.9 us)
Async XLA Ops:
  7.2 229.7 %copy-start = (bf16[20,20]{1,0:T(8,128)(2,1)S(1)}, bf16[20,20]{1,0:T(8,128)(2,1)}, u32[]{:S(2)}) copy-start(bf16[20,20]{1,0:T(8,128)(2,1)} %param.6) | copy-start | bytes 2404
  8.8 11.0 %copy-start.5 = (bf16[9,2,20,20]{3,1,2,0:T(2,128)(2,1)S(1)}, bf16[9,2,20,20]{3,1,2,0:T(2,128)(2,1)}, u32[]{:S(2)}) copy-start(bf16[9,2,20,20]{3,1,2,0:T(2,128)(2,1)} %param.7) | copy-start | bytes 43204
  9.9 122.8 %all-to-all-start = ((bf16[20,32,4,128]{3,2,0,1:T(4,128)(2,1)}), bf16[20,32,4,128]{3,2,0,1:T(4,128)(2,1)}, u32[]{:S(2)}, u32[]{:S(2)}) async-start(bf16[20,32,4,128]{3,2,0,1:T(4,128)(2,1)} %copy.251), calls=%async_computation | async-start | bytes 1310720 | tf_op jit(solution)/shard_map/all_to_all | solution.py:101
  135.2 23.4 %all-to-all-start.1 = ((bf16[20,4,32,128]{3,2,0,1:T(8,128)(2,1)}), bf16[20,4,32,128]{3,2,0,1:T(8,128)(2,1)}, u32[]{:S(2)}, u32[]{:S(2)}) async-start(bf16[20,4,32,128]{3,2,0,1:T(8,128)(2,1)} %copy.254), calls=%async_computation.1 | async-start | bytes 1310720 | tf_op jit(solution)/shard_map/all_to_all | solution.py:100
  140.1 496.3 %all-reduce.3.cloned.1.call-start = ((), (), s32[]{:S(2)}) async-start(), calls=%async_computation.6 | async-start | bytes 11796480
  145.7 6.4 copy-start.1
  161.4 4.8 copy-start.2
  236.3 1.1 copy-start.4
  291.8 2.0 copy-start.3
Sparse Core Ops, SparseCore 0:
  291.9 344.4 all-reduce.2
where the time goes:
time: 714 us
  blocking collectives  385 us (54%)
  waiting for transfers between devices  235 us (33%)
  local copies, waits for them, and re-layouts  40.8 us (6%)
  matrix products  21.4 us (3%)
  between operations  15.1 us (2%)
  starting transfers between devices  14.8 us (2%)
    unnamed x2, waiting for transfers between devices  233 us
    all_gather x1, blocking collectives, local(): lax.all_gather(spectral_weight, ('gx', 'gy'), axis=0, tiled=True)  113 us
    psum x1, blocking collectives, local(): mixing_grad = lax.psum(local_mix, ('dp', 'gx', 'gy')) * mix_scale  107 us
    psum x1, blocking collectives, local(): spectral_grad = lax.psum(share, 'dp') * spec_scale  68.6 us
    all_to_all x1, blocking collectives, to_cells(): lax.all_to_all(lax.all_to_all(plane_block, 'gx', split_axis=2, concat_axi...  39.4 us
    all_to_all x1, blocking collectives, to_planes(): lax.all_to_all(lax.all_to_all(block, 'gx', split_axis=1, concat_axis=2, t...  22.2 us
    all_to_all x1, blocking collectives, to_cells(): lax.all_to_all(plane_block, 'gx', split_axis=2, concat_axis=1, tiled=True)  20.8 us
    unnamed x21, local copies, waits for them, and re-layouts  15.6 us
  transfers between devices with their start and end apart: 3, of which 2 were waited for; matrix products, arithmetic and copies ran while one was open for 3% of the time, Pallas kernels for 0%

commit v1 on v0

--- a/solution.py
+++ b/solution.py
@@ -11,6 +11,7 @@
 P_SIZE = 32
 MODES = 288
 HI = lax.Precision.HIGHEST
+register_zones = lambda link_axis, a_name, field_in: lax.psum(lax.psum(field_in, a_name), link_axis)
 
 
 def gelu_value(h):
@@ -152,7 +153,7 @@
     local_spec = grads_of(spec, gspec)
     share = lax.psum_scatter(local_spec, ("gx", "gy"), scatter_dimension=0, tiled=True)
     spectral_grad = lax.psum(share, "dp") * spec_scale
-    mixing_grad = lax.psum(local_mix, ("dp", "gx", "gy")) * mix_scale
+    mixing_grad = register_zones(("gx", "gy"), "dp", local_mix) * mix_scale
     return (output, spectral_grad, mixing_grad)
 
 

time: 714 us -> 856 us (1.20)
  the two profiles are of different devices: /device:TPU:2 before, /device:TPU:8 now
where the time goes in v1:
time: 856 us; the launch traced here: 855 us
  blocking collectives  418 us (49%)
  waiting for transfers between devices  347 us (41%)
  local copies, waits for them, and re-layouts  40.8 us (5%)
  matrix products  21.4 us (2%)
  between operations  15.1 us (2%)
  starting transfers between devices  11 us (1%)
    unnamed x2, waiting for transfers between devices  347 us
    psum x1, blocking collectives, lax.psum(lax.psum(field_in, a_name), link_axis)  138 us
    all_gather x1, blocking collectives, local(): lax.all_gather(spectral_weight, ('gx', 'gy'), axis=0, tiled=True)  112 us
    psum x1, blocking collectives, local(): spectral_grad = lax.psum(share, 'dp') * spec_scale  67.2 us
    all_to_all x1, blocking collectives, to_cells(): lax.all_to_all(lax.all_to_all(plane_block, 'gx', split_axis=2, concat_axi...  31.7 us
    all_to_all x1, blocking collectives, to_cells(): lax.all_to_all(plane_block, 'gx', split_axis=2, concat_axis=1, tiled=True)  29 us
    all_to_all x1, blocking collectives, to_planes(): lax.all_to_all(lax.all_to_all(block, 'gx', split_axis=1, concat_axis=2, t...  25 us
  transfers between devices with their start and end apart: 3, of which 1 were waited for; matrix products, arithmetic and copies ran while one was open for 2% of the time, Pallas kernels for 0%

profile of v1, /device:TPU:8, one launch (start us, length us, event | category | flops | bytes accessed | tf_op | source)
XLA Modules:
  0.0 854.8 jit_solution(16476314305042747207)
XLA Ops:
  7.2 1.6 reshape_squeeze.3
  8.8 1.1 copy.251
  9.9 4.3 all-to-all-start
  14.2 112.5 %all_gather.3 = bf16[288,2,20,20]{3,1,2,0:T(2,128)(2,1)S(1)} all-gather(bf16[9,2,20,20]{3,1,2,0:T(2,128)(2,1)S(1)} %copy-done.5), channel_id=1, replica_groups=mesh['dp'=16,'gx'=8,'gy'=4] {'gx','gy'}, dimensions={0}, use_global_device_ids=true | all-gather | bytes 475200 | tf_op jit(solution)/shard_map/all_gather | solution.py:142
  126.7 1.3 copy.252
  128.3 0.9 copy.254
  129.2 6.7 all-to-all-start.1
  135.9 5.7 fusion.165
  141.6 6.4 copy.317
  148.0 4.7 copy.318
  152.6 1.2 copy.255
  154.1 0.6 fusion.9
  154.7 0.6 convolution_bitcast_fusion
  155.4 0.9 fusion.33
  156.3 0.9 fusion.29
  157.2 0.9 fusion.15
  158.2 0.9 fusion.14
  160.9 0.4 fusion.41
  162.0 0.4 fusion.12
  162.5 0.4 fusion.13
  162.9 2.2 fusion.24
  165.1 2.2 fusion.8
  167.3 1.3 copy.271
  168.7 29.0 %all_to_all.81 = f32[20,1,128,128]{3,1,0,2:T(1,128)S(1)} all-to-all(f32[20,1,128,128]{3,1,0,2:T(1,128)S(1)} %copy.271), channel_id=1, replica_groups=mesh['dp'=16,'gx'=8,'gy'=4] {'gx'}, dimensions={2} | all-to-all | bytes 2621440 | tf_op jit(solution)/shard_map/all_to_all | solution.py:120
  197.8 0.4 copy.273
  198.2 31.7 %all_to_all.82 = f32[20,8,16,128]{3,1,0,2:T(8,128)S(1)} all-to-all(f32[20,8,16,128]{3,1,0,2:T(8,128)S(1)} %copy.273), channel_id=1, replica_groups=mesh['dp'=16,'gx'=8,'gy'=4] {'gy'}, dimensions={2} | all-to-all | bytes 2621440 | tf_op jit(solution)/shard_map/all_to_all | solution.py:119
  229.9 0.8 copy.357
  230.8 0.5 reshape_reshape.3
  231.3 0.5 copy-done.4
  231.8 4.7 fusion.6
  236.8 14.2 %all_to_all.83 = bf16[20,32,4,128]{3,2,0,1:T(4,128)(2,1)S(1)} all-to-all(bf16[20,32,4,128]{3,2,0,1:T(4,128)(2,1)S(1)} %reshape.261), channel_id=1, replica_groups=mesh['dp'=16,'gx'=8,'gy'=4] {'gx'}, dimensions={1} | all-to-all | bytes 1310720 | tf_op jit(solution)/shard_map/all_to_all | solution.py:102
  251.4 25.0 %all_to_all.84 = bf16[20,4,32,128]{3,2,0,1:T(8,128)(2,1)S(1)} all-to-all(bf16[20,4,32,128]{3,2,0,1:T(8,128)(2,1)S(1)} %copy.282), channel_id=1, replica_groups=mesh['dp'=16,'gx'=8,'gy'=4] {'gy'}, dimensions={1} | all-to-all | bytes 1310720 | tf_op jit(solution)/shard_map/all_to_all | solution.py:101
  276.7 0.6 fusion.59
  277.4 0.6 fusion.63
  278.0 0.9 fusion.27
  278.9 0.9 fusion.35
  279.9 0.9 fusion.11
  280.8 0.9 fusion.10
  283.1 6.0 copy.290
  289.1 1.3 dynamic-slice
  291.1 1.0 copy.292
  292.2 0.7 convolution_bitcast_fusion.1
  292.9 347.3 %all-reduce.4.cloned.1.call-done = f32[288,2,20,20]{3,1,2,0:T(2,128)} async-done(((f32[288,2,20,20]{3,1,2,0:T(2,128)}), f32[288,2,20,20]{3,1,2,0:T(2,128)}) %all-reduce.4.cloned.1.call-update) | async-done | bytes 921616
  640.1 0.9 constant_dynamic-slice_fusion
  641.1 67.2 %all-reduce.1 = (f32[9,2,20,20]{3,1,2,0:T(2,128)S(1)}, f32[20,20]{0,1:T(8,128)S(1)}) all-reduce(f32[9,2,20,20]{3,1,2,0:T(2,128)S(1)} %constant_dynamic-slice_fusion, f32[20,20]{0,1:T(8,128)S(1)} %convolution_bitcast_fusion.1), channel_id=1, replica_groups=mesh['dp'=16,'gx'=8,'gy'=4] {'dp'}, use_global_device_ids=true, to_apply=%region_1.2 | all-reduce | flops 7600 | bytes 60800 | tf_op jit(solution)/shard_map/psum | solution.py:155
  708.3 0.8 broadcast_multiply_fusion
  709.1 138.2 %psum.23 = f32[20,20]{0,1:T(8,128)S(1)} all-reduce(f32[20,20]{0,1:T(8,128)S(1)} %get-tuple-element.34), channel_id=1, replica_groups=mesh['dp'=16,'gx'=8,'gy'=4] {'gx','gy'}, use_global_device_ids=true, to_apply=%region_3.4 | all-reduce | flops 400 | bytes 3200 | tf_op jit(solution)/shard_map/psum | solution.py:14
  847.2 0.7 copy.293
  (50 shorter events, 5.5 us)
Async XLA Ops:
  7.2 224.1 %copy-start = (bf16[20,20]{1,0:T(8,128)(2,1)S(1)}, bf16[20,20]{1,0:T(8,128)(2,1)}, u32[]{:S(2)}) copy-start(bf16[20,20]{1,0:T(8,128)(2,1)} %param.6) | copy-start | bytes 2404
  8.8 5.4 copy-start.5
  9.9 116.8 %all-to-all-start = ((bf16[20,32,4,128]{3,2,0,1:T(4,128)(2,1)}), bf16[20,32,4,128]{3,2,0,1:T(4,128)(2,1)}, u32[]{:S(2)}, u32[]{:S(2)}) async-start(bf16[20,32,4,128]{3,2,0,1:T(4,128)(2,1)} %copy.251), calls=%async_computation | async-start | bytes 1310720 | tf_op jit(solution)/shard_map/all_to_all | solution.py:102
  129.2 23.5 %all-to-all-start.1 = ((bf16[20,4,32,128]{3,2,0,1:T(8,128)(2,1)}), bf16[20,4,32,128]{3,2,0,1:T(8,128)(2,1)}, u32[]{:S(2)}, u32[]{:S(2)}) async-start(bf16[20,4,32,128]{3,2,0,1:T(8,128)(2,1)} %copy.254), calls=%async_computation.1 | async-start | bytes 1310720 | tf_op jit(solution)/shard_map/all_to_all | solution.py:101
  135.9 504.2 %all-reduce.4.cloned.1.call-start = ((), (), s32[]{:S(2)}) async-start(), calls=%async_computation.6 | async-start | bytes 11796480
  141.6 6.4 copy-start.1
  155.4 4.8 copy-start.2
  230.8 1.1 copy-start.4
  289.1 2.0 copy-start.3
Sparse Core Ops, SparseCore 0:
  289.3 350.8 all-reduce.3
